TPU v7x, 32 devices: a whole 2x2x4 slice. The times are simulated.
32 devices in a mesh: dp: 8 (over z, x), ctx: 4 (over y, core).
Axes of the slice: x: 2, y: 2, z: 4, core: 2. Of those that a mesh axis runs over, the one named last changes fastest.
Arguments:
- hidden: bfloat16 [8, 1024, 768], P('dp', 'ctx'), may hold values from -6 to 6
- teacher: bfloat16 [8, 1024, 768], P('dp', 'ctx'), may hold values from -12 to 12
- lengths: int32 [8], P('dp'), may hold values from 256 to 1024, as said below
- w_qkv: bfloat16 [768, 2304], P('dp'), may hold values from -0.21875 to 0.21875
- w_out: bfloat16 [768, 768], P('dp'), may hold values from -0.375 to 0.375
- w_up: bfloat16 [768, 3072], P('dp'), may hold values from -0.375 to 0.375
- w_down: bfloat16 [3072, 768], P('dp'), may hold values from -0.1875 to 0.1875
- norm_gain: bfloat16 [768, 3], P('dp'), may hold values from 0.099609375 to 1.8984375
- norm_shift: bfloat16 [768, 3], P('dp'), may hold values from -3 to 3
- proj_bias: bfloat16 [768, 4], P('dp'), may hold values from -3 to 3
- mid_gain: bfloat16 [3072], P('dp'), may hold values from 0.099609375 to 1.8984375
- mid_shift: bfloat16 [3072], P('dp'), may hold values from -3 to 3
- up_bias: bfloat16 [3072], P('dp'), may hold values from -3 to 3
Outputs:
- layer_output: bfloat16 [8, 1024, 768], P('dp', 'ctx')
- loss: float32 [], replicated
- hidden_grad: float32 [8, 1024, 768], P('dp', 'ctx')
- qkv_grad: float32 [768, 2304], P('dp')
- out_grad: float32 [768, 768], P('dp')
- up_grad: float32 [768, 3072], P('dp')
- down_grad: float32 [3072, 768], P('dp')
- gain_grad: float32 [768, 3], P('dp')
- shift_grad: float32 [768, 3], P('dp')
- bias_grad: float32 [768, 4], P('dp')
- mid_gain_grad: float32 [3072], P('dp')
- mid_shift_grad: float32 [3072], P('dp')
- up_bias_grad: float32 [3072], P('dp')
Inputs may be any that keep to these rules, and one draw needn't show every extreme that they name: Sequence s has valid tokens at positions 0 to lengths[s] - 1 and padding after them; some sequence has exactly 1024 and some exactly 256 valid tokens.
All inputs are finite; a program needn't handle non-finite values.
Results may differ from a plain program's by a relative error of at most 0.013.
Values may be sent and summed in bfloat16 or wider, within the bound.
No kernel may reach another device: no remote copies, remote signals or barrier semaphores. Data moves between devices by JAX's collectives and lax.ppermute only.
A program may use at most 192 MiB of HBM per device.

v0:
```python
import math
import jax
import jax.numpy as jnp
from jax import lax
from jax.sharding import PartitionSpec as P

HEADS = 12
HEAD_DIM = 64
EPSILON = 1e-05
NEGATIVE = -1e30


def passed_along(value, axis, steps):
    count = lax.axis_size(axis)
    pairs = [(source, (source + steps) % count) for source in range(count)]
    return lax.ppermute(value, axis, pairs)


def passed_along_2(block, axis, distance):
    devices = range(lax.axis_size(axis))
    route = [(i - distance, i) for i in devices if i - distance in devices]
    return lax.ppermute(block, axis, route)


def layer_norm(values, gain_vec, shift_vec):
    average = jnp.mean(values, axis=-1, keepdims=True)
    centred = values - average
    variance = jnp.mean(centred * centred, axis=-1, keepdims=True)
    return centred * lax.rsqrt(variance + EPSILON) * gain_vec + shift_vec


def mid_norm(up_proj, gain_vec, shift_vec):
    return layer_norm(jax.nn.gelu(up_proj, approximate=False), gain_vec, shift_vec)


def split_heads(values):
    return values.reshape(values.shape[0], values.shape[1], HEADS, HEAD_DIM)


def key_mask(query_pos, key_start, key_count, lengths):
    key_pos = key_start + jnp.arange(key_count, dtype=jnp.int32)
    causal = key_pos[None, :] <= query_pos[:, None]
    inside = key_pos[None, :] < lengths[:, None]
    return causal[None, :, :] & inside[:, None, :]


def fold_keys(running, pieces, key_start, heads_q, query_pos, lengths):
    row_max, row_total, weighted = running
    key_piece, value_piece = pieces
    key_count = key_piece.shape[1]
    score_scale = 1.0 / math.sqrt(HEAD_DIM)
    scores = (
        jnp.einsum(
            "sqhd,skhd->shqk", heads_q, split_heads(key_piece), preferred_element_type=jnp.float32
        )
        * score_scale
    )
    allowed = key_mask(query_pos, key_start, key_count, lengths)[:, None]
    scores = jnp.where(allowed, scores, NEGATIVE)
    fresh_max = jnp.maximum(row_max, jnp.max(scores, axis=-1))
    exponent_vals = jnp.exp(scores - fresh_max[..., None])
    row_total = jnp.sum(exponent_vals, axis=-1)
    update = jnp.einsum(
        "shqk,skhd->sqhd",
        exponent_vals.astype(jnp.bfloat16),
        split_heads(value_piece),
        preferred_element_type=jnp.float32,
    )
    weighted = update
    return (fresh_max, row_total, weighted)


def grad_keys(
    heads_q, heads_do, log_total, dterm, key_piece, value_piece, key_start, query_pos, lengths
):
    seq_count, key_count = (key_piece.shape[0], key_piece.shape[1])
    heads_k = split_heads(key_piece)
    heads_v = split_heads(value_piece)
    score_scale = 1.0 / math.sqrt(HEAD_DIM)
    scores = (
        jnp.einsum("sqhd,skhd->shqk", heads_q, heads_k, preferred_element_type=jnp.float32)
        * score_scale
    )
    allowed = key_mask(query_pos, key_start, key_count, lengths)[:, None]
    probability = jnp.where(allowed, jnp.exp(scores - log_total[..., None]), 0.0)
    dprob = jnp.einsum("sqhd,skhd->shqk", heads_do, heads_v, preferred_element_type=jnp.float32)
    dscores = (probability * (dprob - dterm[..., None])).astype(jnp.bfloat16)
    dq_part = (
        jnp.einsum("shqk,skhd->sqhd", dscores, heads_k, preferred_element_type=jnp.float32)
        * score_scale
    )
    dk_part = (
        jnp.einsum("shqk,sqhd->skhd", dscores, heads_q, preferred_element_type=jnp.float32)
        * score_scale
    )
    dv_part = jnp.einsum(
        "shqk,sqhd->skhd",
        probability.astype(jnp.bfloat16),
        heads_do,
        preferred_element_type=jnp.float32,
    )
    return (
        dq_part,
        dk_part.reshape(seq_count, key_count, -1),
        dv_part.reshape(seq_count, key_count, -1),
    )


def shards(
    hidden,
    teacher,
    lengths,
    w_qkv,
    w_out,
    w_up,
    w_down,
    norm_gain,
    norm_shift,
    proj_bias,
    mid_gain,
    mid_shift,
    up_bias,
):
    (
        full_qkv,
        full_out,
        full_up,
        full_down,
        gain_full,
        shift_full,
        bias_full,
        mid_gain_full,
        mid_shift_full,
        up_bias_full,
    ) = (
        lax.all_gather(w_qkv, "dp", axis=0, tiled=True),
        lax.all_gather(w_out, "dp", axis=0, tiled=True),
        lax.all_gather(w_up, "dp", axis=0, tiled=True),
        lax.all_gather(w_down, "dp", axis=0, tiled=True),
        lax.all_gather(norm_gain, "dp", axis=0, tiled=True),
        lax.all_gather(norm_shift, "dp", axis=0, tiled=True),
        lax.all_gather(proj_bias, "dp", axis=0, tiled=True),
        lax.all_gather(mid_gain, "dp", axis=0, tiled=True),
        lax.all_gather(mid_shift, "dp", axis=0, tiled=True),
        lax.all_gather(up_bias, "dp", axis=0, tiled=True),
    )
    gain_f = gain_full.astype(jnp.float32)
    shift_f = shift_full.astype(jnp.float32)
    bias_f = bias_full.astype(jnp.float32)
    mid_gain_f = mid_gain_full.astype(jnp.float32)
    mid_shift_f = mid_shift_full.astype(jnp.float32)
    up_bias_f = up_bias_full.astype(jnp.float32)
    seq_count, local_rows, model_width = hidden.shape
    token_rows = seq_count * local_rows
    seq_shape = (seq_count, local_rows, model_width)
    ctx_place = lax.axis_index("ctx")
    ctx_parts = lax.axis_size("ctx")
    query_pos = ctx_place * local_rows + jnp.arange(local_rows, dtype=jnp.int32)
    last_query = ctx_place * local_rows + local_rows - 1
    valid_mask = (query_pos[None, :] < lengths[:, None]).astype(jnp.float32)
    valid_rows = valid_mask.reshape(token_rows, 1)
    hidden_rows = hidden.reshape(token_rows, model_width).astype(jnp.float32)
    normed, pull_in = jax.vjp(layer_norm, hidden_rows, gain_f[:, 0], shift_f[:, 0])
    normed_low = normed.astype(jnp.bfloat16)
    projected = jnp.dot(normed_low, full_qkv, preferred_element_type=jnp.float32)
    query_low = (projected[:, :model_width] + bias_f[:, 0]).astype(jnp.bfloat16).reshape(seq_shape)
    key_low = projected[:, model_width : 2 * model_width].astype(jnp.bfloat16).reshape(seq_shape)
    value_low = (
        (projected[:, 2 * model_width :] + bias_f[:, 1]).astype(jnp.bfloat16).reshape(seq_shape)
    )
    heads_q = split_heads(query_low)
    start_state = (
        jnp.full((seq_count, HEADS, local_rows), NEGATIVE, jnp.float32),
        jnp.zeros((seq_count, HEADS, local_rows), jnp.float32),
        jnp.zeros((seq_count, local_rows, HEADS, HEAD_DIM), jnp.float32),
    )
    pieces = (
        lax.all_gather(key_low, "ctx", axis=1, tiled=True),
        lax.all_gather(value_low, "ctx", axis=1, tiled=True),
    )
    key_start = jnp.int32(0)
    row_max, row_total, weighted = lax.cond(
        key_start <= last_query,
        lambda: fold_keys(start_state, pieces, key_start, heads_q, query_pos, lengths),
        lambda: start_state,
    )
    attended = weighted / jnp.transpose(row_total, (0, 2, 1))[..., None]
    log_total = row_max + jnp.log(row_total)
    attended_rows = attended.reshape(token_rows, model_width)
    mixed, pull_mix = jax.vjp(layer_norm, attended_rows, gain_f[:, 1], shift_f[:, 1])
    mixed_low = mixed.astype(jnp.bfloat16)
    residual = (
        hidden_rows
        + jnp.dot(mixed_low, full_out, preferred_element_type=jnp.float32)
        + bias_f[:, 2]
    )
    ffn_in, pull_ffn = jax.vjp(layer_norm, residual, gain_f[:, 2], shift_f[:, 2])
    ffn_low = ffn_in.astype(jnp.bfloat16)
    up_proj = jnp.dot(ffn_low, full_up, preferred_element_type=jnp.float32) + up_bias_f
    activated, pull_mid = jax.vjp(mid_norm, up_proj, mid_gain_f, mid_shift_f)
    act_low = activated.astype(jnp.bfloat16)
    result = (
        residual + jnp.dot(act_low, full_down, preferred_element_type=jnp.float32) + bias_f[:, 3]
    )
    layer_output = (result * valid_rows).astype(jnp.bfloat16).reshape(hidden.shape)
    error_rows = (
        result - teacher.reshape(token_rows, model_width).astype(jnp.float32)
    ) * valid_rows
    loss_total, valid_total = lax.psum(
        (0.5 * jnp.sum(error_rows * error_rows), jnp.sum(valid_mask)), ("dp", "ctx")
    )
    loss = loss_total / (valid_total * model_width)
    down_low = error_rows.astype(jnp.bfloat16)
    bias_down_grad = jnp.sum(down_low.astype(jnp.float32), axis=0)
    down_grad = jnp.einsum("rf,rd->fd", act_low, down_low, preferred_element_type=jnp.float32)
    d_act = jnp.einsum("rd,fd->rf", down_low, full_down, preferred_element_type=jnp.float32)
    d_up, mid_gain_grad, mid_shift_grad = pull_mid(d_act)
    up_low = d_up.astype(jnp.bfloat16)
    up_bias_grad = jnp.sum(up_low.astype(jnp.float32), axis=0)
    up_grad = jnp.einsum("rd,rf->df", ffn_low, up_low, preferred_element_type=jnp.float32)
    d_ffn = jnp.einsum("rf,df->rd", up_low, full_up, preferred_element_type=jnp.float32)
    d_res_norm, gain_two, shift_two = pull_ffn(d_ffn)
    d_residual = error_rows + d_res_norm
    branch_low = d_residual.astype(jnp.bfloat16)
    bias_out_grad = jnp.sum(branch_low.astype(jnp.float32), axis=0)
    out_grad = jnp.einsum("rd,re->de", mixed_low, branch_low, preferred_element_type=jnp.float32)
    d_mixed = jnp.einsum("re,de->rd", branch_low, full_out, preferred_element_type=jnp.float32)
    d_att, gain_one, shift_one = pull_mix(d_mixed)
    heads_do = split_heads(d_att.astype(jnp.bfloat16).reshape(seq_shape))
    dterm = jnp.einsum("sqhd,sqhd->shq", heads_do.astype(jnp.float32), attended)

    def grad_step(key_piece, value_piece, key_start):
        return grad_keys(
            heads_q,
            heads_do,
            log_total,
            dterm,
            key_piece,
            value_piece,
            key_start,
            query_pos,
            lengths,
        )

    dq_zero = jnp.zeros((seq_count, local_rows, HEADS, HEAD_DIM), jnp.float32)
    own_zero = jnp.zeros(seq_shape, jnp.float32)

    def pass_step(step_index, running):
        key_cur, value_cur, dk_run, dv_run, dq_sum = running
        owner = (ctx_place - step_index) % ctx_parts
        dq_part, dk_part, dv_part = lax.cond(
            owner <= ctx_place,
            lambda: grad_step(key_cur, value_cur, owner * local_rows),
            lambda: (dq_zero, own_zero, own_zero),
        )
        dk_run, dv_run = (
            passed_along((dk_run + dk_part).astype(jnp.bfloat16), "ctx", 1).astype(jnp.float32),
            passed_along((dv_run + dv_part).astype(jnp.bfloat16), "ctx", 1).astype(jnp.float32),
        )
        key_cur, value_cur = passed_along_2((key_cur, value_cur), "ctx", 1)
        return (key_cur, value_cur, dk_run, dv_run, dq_sum + dq_part)

    key_end, value_end, dk_own, dv_own, dq_sum = lax.fori_loop(
        0, ctx_parts, pass_step, (key_low, value_low, own_zero, own_zero, dq_zero)
    )
    dq_low = dq_sum.reshape(token_rows, model_width).astype(jnp.bfloat16)
    dk_low = dk_own.reshape(token_rows, model_width).astype(jnp.bfloat16)
    dv_low = dv_own.reshape(token_rows, model_width).astype(jnp.bfloat16)
    dqkv_low = jnp.concatenate([dq_low, dk_low, dv_low], axis=1)
    bias_q_grad = jnp.sum(dq_low.astype(jnp.float32), axis=0)
    bias_v_grad = jnp.sum(dv_low.astype(jnp.float32), axis=0)
    qkv_grad = jnp.einsum("rd,re->de", normed_low, dqkv_low, preferred_element_type=jnp.float32)
    d_normed = jnp.einsum("re,de->rd", dqkv_low, full_qkv, preferred_element_type=jnp.float32)
    d_in_norm, gain_zero, shift_zero = pull_in(d_normed)
    hidden_grad = (d_residual + d_in_norm).reshape(hidden.shape)
    gain_grad = jnp.stack([gain_zero, gain_one, gain_two], axis=1)
    shift_grad = jnp.stack([shift_zero, shift_one, shift_two], axis=1)
    bias_grad = jnp.stack([bias_q_grad, bias_v_grad, bias_out_grad, bias_down_grad], axis=1)
    shares = (
        lax.psum_scatter(
            qkv_grad.astype(jnp.bfloat16), "dp", scatter_dimension=0, tiled=True
        ).astype(jnp.float32),
        lax.psum_scatter(
            out_grad.astype(jnp.bfloat16), "dp", scatter_dimension=0, tiled=True
        ).astype(jnp.float32),
        lax.psum_scatter(
            up_grad.astype(jnp.bfloat16), "dp", scatter_dimension=0, tiled=True
        ).astype(jnp.float32),
        lax.psum_scatter(
            down_grad.astype(jnp.bfloat16), "dp", scatter_dimension=0, tiled=True
        ).astype(jnp.float32),
        lax.psum_scatter(
            gain_grad.astype(jnp.bfloat16), "dp", scatter_dimension=0, tiled=True
        ).astype(jnp.float32),
        lax.psum_scatter(
            shift_grad.astype(jnp.bfloat16), "dp", scatter_dimension=0, tiled=True
        ).astype(jnp.float32),
        lax.psum_scatter(
            bias_grad.astype(jnp.bfloat16), "dp", scatter_dimension=0, tiled=True
        ).astype(jnp.float32),
        lax.psum_scatter(
            mid_gain_grad.astype(jnp.bfloat16), "dp", scatter_dimension=0, tiled=True
        ).astype(jnp.float32),
        lax.psum_scatter(
            mid_shift_grad.astype(jnp.bfloat16), "dp", scatter_dimension=0, tiled=True
        ).astype(jnp.float32),
        lax.psum_scatter(
            up_bias_grad.astype(jnp.bfloat16), "dp", scatter_dimension=0, tiled=True
        ).astype(jnp.float32),
    )
    summed = (
        lax.psum(shares[0].astype(jnp.bfloat16), "ctx").astype(jnp.float32),
        lax.psum(shares[1].astype(jnp.bfloat16), "ctx").astype(jnp.float32),
        lax.psum(shares[2].astype(jnp.bfloat16), "ctx").astype(jnp.float32),
        lax.psum(shares[3].astype(jnp.bfloat16), "ctx").astype(jnp.float32),
        lax.psum(shares[4].astype(jnp.bfloat16), "ctx").astype(jnp.float32),
        lax.psum(shares[5].astype(jnp.bfloat16), "ctx").astype(jnp.float32),
        lax.psum(shares[6].astype(jnp.bfloat16), "ctx").astype(jnp.float32),
        lax.psum(shares[7].astype(jnp.bfloat16), "ctx").astype(jnp.float32),
        lax.psum(shares[8].astype(jnp.bfloat16), "ctx").astype(jnp.float32),
        lax.psum(shares[9].astype(jnp.bfloat16), "ctx").astype(jnp.float32),
    )
    return (
        layer_output,
        loss,
        hidden_grad,
        summed[0],
        summed[1],
        summed[2],
        summed[3],
        summed[4],
        summed[5],
        summed[6],
        summed[7],
        summed[8],
        summed[9],
    )


def solution(mesh):
    placed = (
        P("dp", "ctx", None),
        P("dp", "ctx", None),
        P("dp"),
        P("dp", None),
        P("dp", None),
        P("dp", None),
        P("dp", None),
        P("dp", None),
        P("dp", None),
        P("dp", None),
        P("dp"),
        P("dp"),
        P("dp"),
    )
    return jax.shard_map(
        shards,
        mesh=mesh,
        in_specs=placed,
        out_specs=(
            P("dp", "ctx", None),
            P(),
            P("dp", "ctx", None),
            P("dp", None),
            P("dp", None),
            P("dp", None),
            P("dp", None),
            P("dp", None),
            P("dp", None),
            P("dp", None),
            P("dp"),
            P("dp"),
            P("dp"),
        ),
        check_vma=False,
    )
```

profile of v0, /device:TPU:0, one launch (start us, length us, event | category | flops | bytes accessed | tf_op | source)
XLA Modules:
  0.0 1042.5 jit_solution(1009641000833723574)
XLA Ops:
  8.0 22.6 %all-gather.3 = bf16[8,96,3]{1,2,0:T(4,128)(2,1)S(1)} all-gather(bf16[1,96,3]{1,2,0:T(4,128)(2,1)} %bitcast.185), channel_id=1, replica_groups=mesh['dp'=8,'ctx'=4] {'dp'}, dimensions={0}, use_global_device_ids=true | all-gather | bytes 5184 | tf_op jit(solution)/shard_map/all_gather | solution.py:141
  30.7 16.6 %all-gather.2 = bf16[8,96,3]{1,2,0:T(4,128)(2,1)S(1)} all-gather(bf16[1,96,3]{1,2,0:T(4,128)(2,1)} %bitcast.186), channel_id=1, replica_groups=mesh['dp'=8,'ctx'=4] {'dp'}, dimensions={0}, use_global_device_ids=true | all-gather | bytes 5184 | tf_op jit(solution)/shard_map/all_gather | solution.py:140
  49.9 28.3 %all-gather.15.cloned.1.call-done = bf16[768,2304]{1,0:T(8,128)(2,1)} async-done(((bf16[96,2304]{1,0:T(8,128)(2,1)}), bf16[768,2304]{1,0:T(8,128)(2,1)}) %all-gather.15.cloned.1.call-update) | async-done | bytes 3538960 | tf_op jit(solution)/shard_map/all_gather | solution.py:136
  78.2 3.3 fusion.73
  82.5 18.1 %all-gather.4 = bf16[8,96,4]{1,2,0:T(4,128)(2,1)S(1)} all-gather(bf16[1,96,4]{1,2,0:T(4,128)(2,1)S(1)} %bitcast.187), channel_id=1, replica_groups=mesh['dp'=8,'ctx'=4] {'dp'}, dimensions={0}, use_global_device_ids=true | all-gather | bytes 6912 | tf_op jit(solution)/shard_map/all_gather | solution.py:142
  104.1 25.9 %all-gather.5 = bf16[8,1,384]{2,1,0:T(2,128)(2,1)S(1)} all-gather(bf16[1,1,384]{2,1,0:T(2,128)(2,1)S(1)} %reshape.470), channel_id=1, replica_groups=mesh['dp'=8,'ctx'=4] {'dp'}, dimensions={0}, use_global_device_ids=true | all-gather | bytes 6912 | tf_op jit(solution)/shard_map/all_gather | solution.py:145
  130.0 26.1 %all-gather.7 = bf16[8,1,384]{2,1,0:T(2,128)(2,1)S(1)} all-gather(bf16[1,1,384]{2,1,0:T(2,128)(2,1)S(1)} %reshape.474), channel_id=1, replica_groups=mesh['dp'=8,'ctx'=4] {'dp'}, dimensions={0}, use_global_device_ids=true | all-gather | bytes 6912 | tf_op jit(solution)/shard_map/all_gather | solution.py:144
  156.1 26.1 %all-gather.6 = bf16[8,1,384]{2,1,0:T(2,128)(2,1)S(1)} all-gather(bf16[1,1,384]{2,1,0:T(2,128)(2,1)S(1)} %reshape.472), channel_id=1, replica_groups=mesh['dp'=8,'ctx'=4] {'dp'}, dimensions={0}, use_global_device_ids=true | all-gather | bytes 6912 | tf_op jit(solution)/shard_map/all_gather | solution.py:143
  185.1 21.4 %conditional.2 = (f32[1,12,256]{2,1,0:T(8,128)}, f32[1,12,256]{2,1,0:T(8,128)}, f32[1,256,12,64]{1,3,2,0:T(8,128)S(1)}, f32[1,12,256]{2,1,0:T(8,128)}) conditional(s32[]{:T(128)} %convert_element_type.247, () %tuple.48, (s32[256]{0:T(256)S(1)}, s32[1]{0:T(128)}, bf16[1,256,12,64]{1,3,2,0:T(8,128)(2,1)}, bf16[1,1024,768]{2,1,0:T(8,128)(2,1)}, ...), branch_computations={%region_2.0_spmd, %region_3.6_spmd} | conditional | flops 840431616 | bytes 106151000 | solution.py:182
  188.3 3.3 fusion.2
  192.3 4.1 fusion.4
  198.1 7.1 fusion.8
  211.1 35.4 %all-gather.19.cloned.1.call-done = bf16[768,3072]{1,0:T(8,128)(2,1)} async-done(((bf16[96,3072]{1,0:T(8,128)(2,1)}), bf16[768,3072]{1,0:T(8,128)(2,1)}) %all-gather.19.cloned.1.call-update) | async-done | bytes 4718608 | tf_op jit(solution)/shard_map/all_gather | solution.py:138
  246.5 12.0 %fusion.85 = (f32[256]{0:T(256)S(1)}, f32[256,3072]{1,0:T(8,128)S(1)}, f32[256,3072]{1,0:T(8,128)}, f32[256,3072]{1,0:T(8,128)}) fusion(f32[3072]{0:T(1024)S(1)} %bitcast.184, bf16[768,3072]{1,0:T(8,128)(2,1)} %all-gather.19.cloned.1.call-done, f32[256,768]{1,0:T(8,128)} %copy-done.6, f32[768]{0:T(1024)S(1)} %get-tuple-element.521, ...), kind=kOutput, calls=%fused_computation.178 | convolution fusion | flops 1260846848 | bytes 14963712 | tf_op jit(solution)/shard_map/dot_general | solution.py:199
  259.0 67.6 %all-gather.21.cloned.1.call-done = bf16[3072,768]{1,0:T(8,128)(2,1)} async-done(((bf16[384,768]{1,0:T(8,128)(2,1)}), bf16[3072,768]{1,0:T(8,128)(2,1)}) %all-gather.21.cloned.1.call-update) | async-done | bytes 4718608 | tf_op jit(solution)/shard_map/all_gather | solution.py:139
  326.6 5.8 convert_reduce_fusion.2
  337.5 3.2 fusion.78
  347.1 2.8 multiply_reduce_fusion.4
  354.7 144.0 %while.24 = (s32[]{:T(128)}, bf16[1,256,768]{1,2,0:T(8,128)(2,1)}, bf16[1,256,768]{1,2,0:T(8,128)(2,1)}, f32[1,256,768]{1,2,0:T(8,128)}, f32[1,256,768]{1,2,0:T(...) while((s32[]{:T(128)}, bf16[1,256,768]{1,2,0:T(8,128)(2,1)}, ...), condition=%wide.region_25.26_spmd.clone, body=%wide.region_22.25_spmd.clone.sunk | while | flops 513672192 | bytes 48655496 | solution.py:263
  358.2 14.6 %conditional.5 = (f32[1,256,12,64]{1,3,2,0:T(8,128)}, f32[1,256,768]{1,2,0:T(8,128)}, f32[1,256,768]{1,2,0:T(8,128)}) conditional(s32[]{:T(128)} %convert_element_type.407, () %tuple.115, (s32[]{:T(128)}, s32[]{:T(128)}, s32[1]{0:T(128)}, bf16[1,256,12,64]{1,3,2,0:T(8,128)(2,1)}, bf16[1,256,768]{1,2,0:T(8,128)(2,1)S(1)}, ...), branch_computations={%region_23.23_spmd, %region_24.24_spmd} | conditional | flops 511706112 | bytes 32138860 | solution.py:251
  358.2 3.3 fusion.28
  362.9 3.5 multiply_convert_fusion
  370.2 2.7 fusion.18
  378.4 2.7 collective-permute-start
  393.0 2.8 conditional.5
  398.0 16.3 %collective-permute-start.2 = (bf16[1,256,768]{1,2,0:T(8,128)(2,1)}, bf16[1,256,768]{1,2,0:T(8,128)(2,1)}, u32[]{:S(2)}, u32[]{:S(2)}) collective-permute-start(bf16[1,256,768]{1,2,0:T(8,128)(2,1)} %fusion.110), channel_id=1, source_target_pairs={{0,1},{1,2},{2,3},{3,0},{4,5},{5,6},{6,7},{7,4},{8,9},{9,10},{10,1... | collective-permute-start | bytes 1179656 | tf_op jit(solution)/shard_map/while/body/eval_jaxpr/ppermute | solution.py:16
  418.9 2.7 collective-permute-start
  433.2 2.8 conditional.5
  438.3 4.5 collective-permute-start.2
  445.0 14.2 %collective-permute-start.3 = (bf16[1,256,768]{1,2,0:T(8,128)(2,1)}, bf16[1,256,768]{1,2,0:T(8,128)(2,1)}, u32[]{:S(2)}, u32[]{:S(2)}) collective-permute-start(bf16[1,256,768]{1,2,0:T(8,128)(2,1)} %fusion.111), channel_id=1, source_target_pairs={{0,1},{1,2},{2,3},{3,0},{4,5},{5,6},{6,7},{7,4},{8,9},{9,10},{10,1... | collective-permute-start | bytes 1179656 | tf_op jit(solution)/shard_map/while/body/eval_jaxpr/ppermute | solution.py:16
  459.2 2.7 collective-permute-start
  473.5 2.8 conditional.5
  478.5 4.5 collective-permute-start.2
  487.7 2.7 collective-permute-start
  504.1 3.1 convolution_convert_fusion.2
  507.3 5.4 convolution_convert_fusion.1
  513.3 5.1 convolution_convert_fusion
  519.7 3.9 fusion.77
  541.5 48.6 %reduce-scatter.14.cloned.1.call-done = bf16[96,2304]{1,0:T(8,128)(2,1)} async-done(((bf16[768,2304]{1,0:T(8,128)(2,1)}), bf16[96,2304]{1,0:T(8,128)(2,1)}) %reduce-scatter.14.cloned.1.call-update) | async-done | bytes 442384 | tf_op jit(solution)/shard_map/reduce_scatter | solution.py:280
  590.1 98.8 %reduce-scatter.18.cloned.1.call-done = bf16[96,3072]{1,0:T(8,128)(2,1)} async-done(((bf16[768,3072]{1,0:T(8,128)(2,1)}), bf16[96,3072]{1,0:T(8,128)(2,1)}) %reduce-scatter.18.cloned.1.call-update) | async-done | bytes 589840 | tf_op jit(solution)/shard_map/reduce_scatter | solution.py:286
  689.0 98.5 %reduce-scatter.20.cloned.1.call-done = bf16[384,768]{1,0:T(8,128)(2,1)} async-done(((bf16[3072,768]{1,0:T(8,128)(2,1)}), bf16[384,768]{1,0:T(8,128)(2,1)}) %reduce-scatter.20.cloned.1.call-update) | async-done | bytes 589840 | tf_op jit(solution)/shard_map/reduce_scatter | solution.py:289
  790.1 2.6 add_bitcast_fusion
  793.9 40.5 %all-reduce.3 = (f32[]{:T(128)}, f32[]{:T(128)}) all-reduce(f32[]{:T(128)S(6)} %mul.346, f32[]{:T(128)} %fusion.71), channel_id=1, replica_groups=mesh['dp'=8,'ctx'=4] {'dp','ctx'}, use_global_device_ids=true, to_apply=%region_13.14 | all-reduce | flops 2 | bytes 16 | tf_op jit(solution)/shard_map/psum | solution.py:209
  834.5 36.7 %all-reduce.4 = (bf16[3072]{0:T(1024)(128)(2,1)S(1)}, bf16[3072]{0:T(1024)(128)(2,1)S(1)}, bf16[3072]{0:T(1024)(128)(2,1)S(1)}) all-reduce(bf16[3072]{0:T(1024)(128)(2,1)} %get-tuple-element.504, bf16[3072]{0:T(1024)(128)(2,1)} %get-tuple-element.506, bf16[3072]{0:T(1024)(128)(2,1)S(1)} %copy-done.41), channel_id=11, replica_groups=mesh['dp'=8,'ctx'=4] {'dp'}, use_global_device_ids=true, to_apply=%region_53.54.clone | all-reduce | flops 9216 | bytes 36864
  875.0 41.1 %reduce-scatter.24.cloned.1.call-done = bf16[96,3]{1,0:T(8,128)(2,1)} async-done(((bf16[768,3]{1,0:T(8,128)(2,1)}), bf16[96,3]{1,0:T(8,128)(2,1)}) %reduce-scatter.24.cloned.1.call-update) | async-done | bytes 592
  916.9 62.6 %reduce-scatter.26.cloned.1.call-done = bf16[96,4]{1,0:T(8,128)(2,1)} async-done(((bf16[768,4]{1,0:T(8,128)(2,1)}), bf16[96,4]{1,0:T(8,128)(2,1)}) %reduce-scatter.26.cloned.1.call-update) | async-done | bytes 784
  980.3 5.7 all-reduce.5
  989.5 38.1 %all-reduce.9.cloned.1.call-done = (bf16[96,2304]{1,0:T(8,128)(2,1)}, bf16[96,768]{1,0:T(8,128)(2,1)}, bf16[96,3072]{1,0:T(8,128)(2,1)}, bf16[384,768]{1,0:T(8,128)(2,1)}) async-done(((bf16[96,2304]{1,0:T(8,128)(2,1)}, bf16[96,768]{1,0:T(8,128)(2,1)}, bf16[96,3072]{1,0:T(8,128)(2,1)}, bf16[384,768]{1,0:T(8,128)(2,1)}), (bf16[96,2304]{1,0:T(8,128)(2,1)}, bf16[96,768]{1,0:T(8,128)(2,1)}, ...) | async-done | bytes 1769488 | tf_op jit(solution)/shard_map/psum | solution.py:312
  (360 shorter events, 164.0 us)
Async XLA Ops:
  7.2 71.0 %all-gather.15.cloned.1.call-start = ((), (), s32[]{:S(2)}) async-start(), calls=%async_computation.7 | async-start | bytes 3981312 | tf_op jit(solution)/shard_map/all_gather | solution.py:136
  7.9 177.2 %all-gather.23.cloned.1.call-start = ((), (), s32[]{:S(2)}) async-start(), calls=%async_computation.15 | async-start | bytes 1966080 | tf_op jit(solution)/shard_map/all_gather | solution.py:178
  47.4 160.5 %copy-start.33 = (f32[768]{0:T(1024)}, f32[768]{0:T(1024)S(1)}, u32[]{:S(2)}) copy-start(f32[768]{0:T(1024)S(1)} %get-tuple-element.605) | copy-start | bytes 9220
  47.4 160.5 %copy-start.48 = (f32[768]{0:T(1024)}, f32[768]{0:T(1024)S(1)}, u32[]{:S(2)}) copy-start(f32[768]{0:T(1024)S(1)} %get-tuple-element.522) | copy-start | bytes 9220
  47.4 199.0 %copy-start.32 = (f32[768]{0:T(1024)}, f32[768]{0:T(1024)S(1)}, u32[]{:S(2)}) copy-start(f32[768]{0:T(1024)S(1)} %get-tuple-element.521) | copy-start | bytes 9220
  81.6 48.4 %copy-start.71 = (bf16[384]{0:T(512)(128)(2,1)S(1)}, bf16[384]{0:T(512)(128)(2,1)}, u32[]{:S(2)}) copy-start(bf16[384]{0:T(512)(128)(2,1)} %param.30) | copy-start | bytes 2308
  81.6 74.5 %copy-start.72 = (bf16[384]{0:T(512)(128)(2,1)S(1)}, bf16[384]{0:T(512)(128)(2,1)}, u32[]{:S(2)}) copy-start(bf16[384]{0:T(512)(128)(2,1)} %param.29) | copy-start | bytes 2308
  82.4 102.7 %all-gather.25.cloned.1.call-start = ((), (), s32[]{:S(2)}) async-start(), calls=%async_computation.16 | async-start | bytes 1966080 | tf_op jit(solution)/shard_map/all_gather | solution.py:179
  101.6 82.7 %copy-start.17 = (bf16[256,768]{1,0:T(8,128)(2,1)S(1)}, bf16[256,768]{1,0:T(8,128)(2,1)}, u32[]{:S(2)}) copy-start(bf16[256,768]{1,0:T(8,128)(2,1)} %get-tuple-element.592) | copy-start | bytes 1179652
  101.6 106.4 %all-gather.17.cloned.1.call-start = ((), (), s32[]{:S(2)}) async-start(), calls=%async_computation.8 | async-start | bytes 1327104 | tf_op jit(solution)/shard_map/all_gather | solution.py:137
  102.2 144.3 %all-gather.19.cloned.1.call-start = ((), (), s32[]{:S(2)}) async-start(), calls=%async_computation.9 | async-start | bytes 5308416 | tf_op jit(solution)/shard_map/all_gather | solution.py:138
  102.7 223.8 %all-gather.21.cloned.1.call-start = ((), (), s32[]{:S(2)}) async-start(), calls=%async_computation.10 | async-start | bytes 5308416 | tf_op jit(solution)/shard_map/all_gather | solution.py:139
  103.3 438.2 %reduce-scatter.16.cloned.1.call-start = ((), (), s32[]{:S(2)}) async-start(), calls=%async_computation.12 | async-start | bytes 1327104 | tf_op jit(solution)/shard_map/reduce_scatter | solution.py:283
  156.1 170.4 %copy-start.29 = (f32[8,1,384]{2,1,0:T(1,128)}, f32[8,1,384]{2,1,0:T(1,128)S(1)}, u32[]{:S(2)}) copy-start(f32[8,1,384]{2,1,0:T(1,128)S(1)} %convert_element_type.300) | copy-start | bytes 36868
  182.3 144.3 %copy-start.66 = (f32[256]{0:T(256)}, f32[256]{0:T(256)S(1)}, u32[]{:S(2)}) copy-start(f32[256]{0:T(256)S(1)} %compare_convert_fusion) | copy-start | bytes 3076
  207.7 38.7 %copy-start.10 = (f32[256,768]{1,0:T(8,128)}, f32[256,768]{1,0:T(8,128)S(1)}, u32[]{:S(2)}) copy-start(f32[256,768]{1,0:T(8,128)S(1)} %copy.62) | copy-start | bytes 2359300
  207.8 50.7 %copy-start.45 = (f32[256]{0:T(256)}, f32[256]{0:T(256)S(1)}, u32[]{:S(2)}) copy-start(f32[256]{0:T(256)S(1)} %broadcast_multiply_fusion.2) | copy-start | bytes 3076
  210.0 134.1 %copy-start.40 = (f32[256]{0:T(256)}, f32[256]{0:T(256)S(1)}, u32[]{:S(2)}) copy-start(f32[256]{0:T(256)S(1)} %broadcast_multiply_fusion.1) | copy-start | bytes 3076
  211.1 133.0 %copy-start.51 = (f32[256]{0:T(256)}, f32[256]{0:T(256)S(1)}, u32[]{:S(2)}) copy-start(f32[256]{0:T(256)S(1)} %fusion.64) | copy-start | bytes 3076
  258.5 78.1 %copy-start.30 = (f32[256]{0:T(256)}, f32[256]{0:T(256)S(1)}, u32[]{:S(2)}) copy-start(f32[256]{0:T(256)S(1)} %broadcast_multiply_fusion) | copy-start | bytes 3076
  258.9 77.6 %copy-start.39 = (f32[256]{0:T(256)}, f32[256]{0:T(256)S(1)}, u32[]{:S(2)}) copy-start(f32[256]{0:T(256)S(1)} %fusion.65) | copy-start | bytes 3076
  353.3 236.9 %reduce-scatter.14.cloned.1.call-start = ((), (), s32[]{:S(2)}) async-start(), calls=%async_computation.11 | async-start | bytes 3981312 | tf_op jit(solution)/shard_map/reduce_scatter | solution.py:280
  374.8 11.0 %collective-permute-start.2 = (bf16[1,256,768]{1,2,0:T(8,128)(2,1)}, bf16[1,256,768]{1,2,0:T(8,128)(2,1)}, u32[]{:S(2)}, u32[]{:S(2)}) collective-permute-start(bf16[1,256,768]{1,2,0:T(8,128)(2,1)} %fusion.110), channel_id=1, source_target_pairs={{0,1},{1,2},{2,3},{3,0},{4,5},{5,6},{6,7},{7,4},{8,9},{9,10},{10,1... | collective-permute-start | bytes 1179656 | tf_op jit(solution)/shard_map/while/body/eval_jaxpr/ppermute | solution.py:16
  376.8 10.9 %collective-permute-start.3 = (bf16[1,256,768]{1,2,0:T(8,128)(2,1)}, bf16[1,256,768]{1,2,0:T(8,128)(2,1)}, u32[]{:S(2)}, u32[]{:S(2)}) collective-permute-start(bf16[1,256,768]{1,2,0:T(8,128)(2,1)} %fusion.111), channel_id=1, source_target_pairs={{0,1},{1,2},{2,3},{3,0},{4,5},{5,6},{6,7},{7,4},{8,9},{9,10},{10,1... | collective-permute-start | bytes 1179656 | tf_op jit(solution)/shard_map/while/body/eval_jaxpr/ppermute | solution.py:16
  378.4 11.2 %collective-permute-start = (bf16[1,256,768]{1,2,0:T(8,128)(2,1)S(1)}, bf16[1,256,768]{1,2,0:T(8,128)(2,1)}, u32[]{:S(2)}, u32[]{:S(2)}) collective-permute-start(bf16[1,256,768]{1,2,0:T(8,128)(2,1)S(1)} %copy.106), channel_id=1, source_target_pairs={{0,1},{1,2},{2,3},{4,5},{5,6},{6,7},{8,9},{9,10},{10,11},{12,13},{... | collective-permute-start | bytes 1179656 | tf_op jit(solution)/shard_map/while/body/eval_jaxpr/ppermute | solution.py:22
  381.1 8.5 collective-permute-start.1
  398.0 28.0 %collective-permute-start.2 = (bf16[1,256,768]{1,2,0:T(8,128)(2,1)}, bf16[1,256,768]{1,2,0:T(8,128)(2,1)}, u32[]{:S(2)}, u32[]{:S(2)}) collective-permute-start(bf16[1,256,768]{1,2,0:T(8,128)(2,1)} %fusion.110), channel_id=1, source_target_pairs={{0,1},{1,2},{2,3},{3,0},{4,5},{5,6},{6,7},{7,4},{8,9},{9,10},{10,1... | collective-permute-start | bytes 1179656 | tf_op jit(solution)/shard_map/while/body/eval_jaxpr/ppermute | solution.py:16
  416.6 11.4 %collective-permute-start.3 = (bf16[1,256,768]{1,2,0:T(8,128)(2,1)}, bf16[1,256,768]{1,2,0:T(8,128)(2,1)}, u32[]{:S(2)}, u32[]{:S(2)}) collective-permute-start(bf16[1,256,768]{1,2,0:T(8,128)(2,1)} %fusion.111), channel_id=1, source_target_pairs={{0,1},{1,2},{2,3},{3,0},{4,5},{5,6},{6,7},{7,4},{8,9},{9,10},{10,1... | collective-permute-start | bytes 1179656 | tf_op jit(solution)/shard_map/while/body/eval_jaxpr/ppermute | solution.py:16
  418.9 11.0 %collective-permute-start = (bf16[1,256,768]{1,2,0:T(8,128)(2,1)S(1)}, bf16[1,256,768]{1,2,0:T(8,128)(2,1)}, u32[]{:S(2)}, u32[]{:S(2)}) collective-permute-start(bf16[1,256,768]{1,2,0:T(8,128)(2,1)S(1)} %copy.106), channel_id=1, source_target_pairs={{0,1},{1,2},{2,3},{4,5},{5,6},{6,7},{8,9},{9,10},{10,11},{12,13},{... | collective-permute-start | bytes 1179656 | tf_op jit(solution)/shard_map/while/body/eval_jaxpr/ppermute | solution.py:22
  421.6 8.3 collective-permute-start.1
  438.3 28.0 %collective-permute-start.2 = (bf16[1,256,768]{1,2,0:T(8,128)(2,1)}, bf16[1,256,768]{1,2,0:T(8,128)(2,1)}, u32[]{:S(2)}, u32[]{:S(2)}) collective-permute-start(bf16[1,256,768]{1,2,0:T(8,128)(2,1)} %fusion.110), channel_id=1, source_target_pairs={{0,1},{1,2},{2,3},{3,0},{4,5},{5,6},{6,7},{7,4},{8,9},{9,10},{10,1... | collective-permute-start | bytes 1179656 | tf_op jit(solution)/shard_map/while/body/eval_jaxpr/ppermute | solution.py:16
  445.0 23.2 %collective-permute-start.3 = (bf16[1,256,768]{1,2,0:T(8,128)(2,1)}, bf16[1,256,768]{1,2,0:T(8,128)(2,1)}, u32[]{:S(2)}, u32[]{:S(2)}) collective-permute-start(bf16[1,256,768]{1,2,0:T(8,128)(2,1)} %fusion.111), channel_id=1, source_target_pairs={{0,1},{1,2},{2,3},{3,0},{4,5},{5,6},{6,7},{7,4},{8,9},{9,10},{10,1... | collective-permute-start | bytes 1179656 | tf_op jit(solution)/shard_map/while/body/eval_jaxpr/ppermute | solution.py:16
  459.2 10.9 %collective-permute-start = (bf16[1,256,768]{1,2,0:T(8,128)(2,1)S(1)}, bf16[1,256,768]{1,2,0:T(8,128)(2,1)}, u32[]{:S(2)}, u32[]{:S(2)}) collective-permute-start(bf16[1,256,768]{1,2,0:T(8,128)(2,1)S(1)} %copy.106), channel_id=1, source_target_pairs={{0,1},{1,2},{2,3},{4,5},{5,6},{6,7},{8,9},{9,10},{10,11},{12,13},{... | collective-permute-start | bytes 1179656 | tf_op jit(solution)/shard_map/while/body/eval_jaxpr/ppermute | solution.py:22
  461.9 8.3 collective-permute-start.1
  478.5 16.3 %collective-permute-start.2 = (bf16[1,256,768]{1,2,0:T(8,128)(2,1)}, bf16[1,256,768]{1,2,0:T(8,128)(2,1)}, u32[]{:S(2)}, u32[]{:S(2)}) collective-permute-start(bf16[1,256,768]{1,2,0:T(8,128)(2,1)} %fusion.110), channel_id=1, source_target_pairs={{0,1},{1,2},{2,3},{3,0},{4,5},{5,6},{6,7},{7,4},{8,9},{9,10},{10,1... | collective-permute-start | bytes 1179656 | tf_op jit(solution)/shard_map/while/body/eval_jaxpr/ppermute | solution.py:16
  485.2 11.5 %collective-permute-start.3 = (bf16[1,256,768]{1,2,0:T(8,128)(2,1)}, bf16[1,256,768]{1,2,0:T(8,128)(2,1)}, u32[]{:S(2)}, u32[]{:S(2)}) collective-permute-start(bf16[1,256,768]{1,2,0:T(8,128)(2,1)} %fusion.111), channel_id=1, source_target_pairs={{0,1},{1,2},{2,3},{3,0},{4,5},{5,6},{6,7},{7,4},{8,9},{9,10},{10,1... | collective-permute-start | bytes 1179656 | tf_op jit(solution)/shard_map/while/body/eval_jaxpr/ppermute | solution.py:16
  487.7 10.9 %collective-permute-start = (bf16[1,256,768]{1,2,0:T(8,128)(2,1)S(1)}, bf16[1,256,768]{1,2,0:T(8,128)(2,1)}, u32[]{:S(2)}, u32[]{:S(2)}) collective-permute-start(bf16[1,256,768]{1,2,0:T(8,128)(2,1)S(1)} %copy.106), channel_id=1, source_target_pairs={{0,1},{1,2},{2,3},{4,5},{5,6},{6,7},{8,9},{9,10},{10,11},{12,13},{... | collective-permute-start | bytes 1179656 | tf_op jit(solution)/shard_map/while/body/eval_jaxpr/ppermute | solution.py:22
  490.4 8.3 collective-permute-start.1
  507.2 181.7 %reduce-scatter.18.cloned.1.call-start = ((), (), s32[]{:S(2)}) async-start(), calls=%async_computation.13 | async-start | bytes 5308416 | tf_op jit(solution)/shard_map/reduce_scatter | solution.py:286
  512.7 274.8 %reduce-scatter.20.cloned.1.call-start = ((), (), s32[]{:S(2)}) async-start(), calls=%async_computation.14 | async-start | bytes 5308416 | tf_op jit(solution)/shard_map/reduce_scatter | solution.py:289
  518.5 355.8 %reduce-scatter.22.cloned.1.call-start = ((), (), s32[]{:S(2)}) async-start(), calls=%async_computation.17 | async-start | bytes 221184
  523.6 266.5 %copy-start.5 = (f32[256,768]{1,0:T(8,128)S(1)}, f32[256,768]{1,0:T(8,128)}, u32[]{:S(2)}) copy-start(f32[256,768]{1,0:T(8,128)} %copy-done.4) | copy-start | bytes 2359300
  523.6 266.5 %copy-start.9 = (f32[256,768]{1,0:T(8,128)S(1)}, f32[256,768]{1,0:T(8,128)}, u32[]{:S(2)}) copy-start(f32[256,768]{1,0:T(8,128)} %copy-done.8) | copy-start | bytes 2359300
  530.1 304.4 %copy-start.41 = (bf16[3072]{0:T(1024)(128)(2,1)S(1)}, bf16[3072]{0:T(1024)(128)(2,1)}, u32[]{:S(2)}) copy-start(bf16[3072]{0:T(1024)(128)(2,1)} %get-tuple-element.569) | copy-start | bytes 18436
  530.1 342.6 %copy-start.21 = (f32[256,768]{1,0:T(8,128)S(1)}, f32[256,768]{1,0:T(8,128)}, u32[]{:S(2)}) copy-start(f32[256,768]{1,0:T(8,128)} %get-tuple-element.599) | copy-start | bytes 2359300
  530.1 386.0 %reduce-scatter.24.cloned.1.call-start = ((), (), s32[]{:S(2)}) async-start(), calls=%async_computation.18 | async-start | bytes 221184
  538.2 441.3 %reduce-scatter.26.cloned.1.call-start = ((), (), s32[]{:S(2)}) async-start(), calls=%async_computation.19 | async-start | bytes 221184
  541.2 486.4 %all-reduce.9.cloned.1.call-start = ((), (), s32[]{:S(2)}) async-start(), calls=%async_computation.20 | async-start | bytes 3538944 | tf_op jit(solution)/shard_map/psum | solution.py:312
  (57 other events, 345.3 us)
Sparse Core Ops, SparseCore 0:
  10.2 67.9 all-gather.14
  82.5 18.1 all-gather.22
  102.9 19.6 all-gather.24
  124.6 41.1 all-gather.16
  167.8 78.6 all-gather.18
  248.5 78.0 all-gather.20
  353.4 62.2 reduce-scatter.15
  507.4 82.7 reduce-scatter.13
  593.8 95.1 reduce-scatter.17
  692.5 94.9 reduce-scatter.19
  791.4 60.8 reduce-scatter.21
  856.0 60.0 reduce-scatter.23
  919.4 60.0 reduce-scatter.25
  982.0 45.6 all-reduce.8
where the time goes:
time: 1050 us; the launch traced here: 1040 us
  waiting for transfers between devices  522 us (50%)
  blocking collectives  218 us (21%)
  other arithmetic  88.9 us (8%)
  matrix products  73 us (7%)
  starting transfers between devices  66.2 us (6%)
  local copies, waits for them, and re-layouts  54.6 us (5%)
  between operations  19.5 us (2%)
    unnamed x17, waiting for transfers between devices  106 us
    reduce_scatter x1, waiting for transfers between devices, shards(): lax.psum_scatter(up_grad.astype(jnp.bfloat16), 'dp', scatter_dimension=0,...  98.8 us
    reduce_scatter x1, waiting for transfers between devices, shards(): lax.psum_scatter(down_grad.astype(jnp.bfloat16), 'dp', scatter_dimension=...  98.5 us
    all_gather x1, waiting for transfers between devices, shards(): lax.all_gather(w_down, 'dp', axis=0, tiled=True)  67.6 us
    reduce_scatter x1, waiting for transfers between devices, shards(): lax.psum_scatter(qkv_grad.astype(jnp.bfloat16), 'dp', scatter_dimension=0...  48.6 us
    ppermute x8, starting transfers between devices, passed_along(): return lax.ppermute(value, axis, pairs)  46.1 us
    psum x1, blocking collectives, shards(): lax.psum((0.5 * jnp.sum(error_rows * error_rows), jnp.sum(valid_mask)), (...  40.5 us
    psum x1, waiting for transfers between devices, shards(): lax.psum(shares[0].astype(jnp.bfloat16), 'ctx').astype(jnp.float32)  38.1 us
  transfers between devices with their start and end apart: 30, of which 9 were waited for; matrix products, arithmetic and copies ran while one was open for 17% of the time, Pallas kernels for 0%

commit v1 on v0

--- a/solution.py
+++ b/solution.py
@@ -8,6 +8,12 @@
 HEAD_DIM = 64
 EPSILON = 1e-05
 NEGATIVE = -1e30
+
+
+def gather_and_add(shard, axis):
+    terms = lax.all_gather(shard, axis, axis=0, tiled=False)
+    acc = terms.sum(axis=0)
+    return acc
 
 
 def passed_along(value, axis, steps):
@@ -309,7 +315,7 @@
         ).astype(jnp.float32),
     )
     summed = (
-        lax.psum(shares[0].astype(jnp.bfloat16), "ctx").astype(jnp.float32),
+        gather_and_add(shares[0].astype(jnp.bfloat16), "ctx").astype(jnp.float32),
         lax.psum(shares[1].astype(jnp.bfloat16), "ctx").astype(jnp.float32),
         lax.psum(shares[2].astype(jnp.bfloat16), "ctx").astype(jnp.float32),
         lax.psum(shares[3].astype(jnp.bfloat16), "ctx").astype(jnp.float32),

time: 1050 us -> 1130 us (1.076)
  waiting for transfers between devices: 522 us -> 599 us
    reduce_scatter x1, waiting for transfers between devices: 0.02 us -> 65.6 us  [shards(): lax.psum_scatter(out_grad.astype(jnp.bfloat16), 'dp', scatter_dimension=0...]
    unnamed x17 -> x18, waiting for transfers between devices: 106 us -> 108 us
  transfers between devices with their start and end apart: 30 -> 31, of which waited for: 9 -> 11; matrix products, arithmetic and copies ran while one was open for 17% -> 11% of each run, Pallas kernels for 0% -> 0%
where the time goes in v1:
time: 1130 us; the launch traced here: 1120 us
  waiting for transfers between devices  599 us (53%)
  blocking collectives  219 us (19%)
  other arithmetic  90.5 us (8%)
  matrix products  72.7 us (6%)
  starting transfers between devices  66.3 us (6%)
  local copies, waits for them, and re-layouts  54.9 us (5%)
  between operations  19.4 us (2%)
    unnamed x18, waiting for transfers between devices  108 us
    reduce_scatter x1, waiting for transfers between devices, shards(): lax.psum_scatter(down_grad.astype(jnp.bfloat16), 'dp', scatter_dimension=...  98.5 us
    reduce_scatter x1, waiting for transfers between devices, shards(): lax.psum_scatter(up_grad.astype(jnp.bfloat16), 'dp', scatter_dimension=0,...  98.5 us
    all_gather x1, waiting for transfers between devices, shards(): lax.all_gather(w_down, 'dp', axis=0, tiled=True)  67.3 us
    reduce_scatter x1, waiting for transfers between devices, shards(): lax.psum_scatter(out_grad.astype(jnp.bfloat16), 'dp', scatter_dimension=0...  65.6 us
    ppermute x8, starting transfers between devices, passed_along(): return lax.ppermute(value, axis, pairs)  46.2 us
    reduce_scatter x1, waiting for transfers between devices, shards(): lax.psum_scatter(qkv_grad.astype(jnp.bfloat16), 'dp', scatter_dimension=0...  45.7 us
    psum x1, blocking collectives, shards(): lax.psum((0.5 * jnp.sum(error_rows * error_rows), jnp.sum(valid_mask)), (...  40.6 us
  transfers between devices with their start and end apart: 31, of which 11 were waited for; matrix products, arithmetic and copies ran while one was open for 11% of the time, Pallas kernels for 0%

profile of v1, /device:TPU:0, one launch (start us, length us, event | category | flops | bytes accessed | tf_op | source)
XLA Modules:
  0.0 1121.2 jit_solution(5382936814092778545)
XLA Ops:
  8.0 22.6 %all-gather.4 = bf16[8,96,3]{1,2,0:T(4,128)(2,1)S(1)} all-gather(bf16[1,96,3]{1,2,0:T(4,128)(2,1)} %bitcast.187), channel_id=1, replica_groups=mesh['dp'=8,'ctx'=4] {'dp'}, dimensions={0}, use_global_device_ids=true | all-gather | bytes 5184 | tf_op jit(solution)/shard_map/all_gather | solution.py:147
  30.7 16.6 %all-gather.3 = bf16[8,96,3]{1,2,0:T(4,128)(2,1)S(1)} all-gather(bf16[1,96,3]{1,2,0:T(4,128)(2,1)} %bitcast.188), channel_id=1, replica_groups=mesh['dp'=8,'ctx'=4] {'dp'}, dimensions={0}, use_global_device_ids=true | all-gather | bytes 5184 | tf_op jit(solution)/shard_map/all_gather | solution.py:146
  49.9 28.3 %all-gather.17.cloned.1.call-done = bf16[768,2304]{1,0:T(8,128)(2,1)} async-done(((bf16[96,2304]{1,0:T(8,128)(2,1)}), bf16[768,2304]{1,0:T(8,128)(2,1)}) %all-gather.17.cloned.1.call-update) | async-done | bytes 3538960 | tf_op jit(solution)/shard_map/all_gather | solution.py:142
  78.2 3.3 fusion.73
  82.5 18.1 %all-gather.5 = bf16[8,96,4]{1,2,0:T(4,128)(2,1)S(1)} all-gather(bf16[1,96,4]{1,2,0:T(4,128)(2,1)S(1)} %bitcast.189), channel_id=1, replica_groups=mesh['dp'=8,'ctx'=4] {'dp'}, dimensions={0}, use_global_device_ids=true | all-gather | bytes 6912 | tf_op jit(solution)/shard_map/all_gather | solution.py:148
  104.1 25.9 %all-gather.6 = bf16[8,1,384]{2,1,0:T(2,128)(2,1)S(1)} all-gather(bf16[1,1,384]{2,1,0:T(2,128)(2,1)S(1)} %reshape.471), channel_id=1, replica_groups=mesh['dp'=8,'ctx'=4] {'dp'}, dimensions={0}, use_global_device_ids=true | all-gather | bytes 6912 | tf_op jit(solution)/shard_map/all_gather | solution.py:151
  130.0 26.1 %all-gather.8 = bf16[8,1,384]{2,1,0:T(2,128)(2,1)S(1)} all-gather(bf16[1,1,384]{2,1,0:T(2,128)(2,1)S(1)} %reshape.475), channel_id=1, replica_groups=mesh['dp'=8,'ctx'=4] {'dp'}, dimensions={0}, use_global_device_ids=true | all-gather | bytes 6912 | tf_op jit(solution)/shard_map/all_gather | solution.py:150
  156.1 26.3 %all-gather.7 = bf16[8,1,384]{2,1,0:T(2,128)(2,1)S(1)} all-gather(bf16[1,1,384]{2,1,0:T(2,128)(2,1)S(1)} %reshape.473), channel_id=1, replica_groups=mesh['dp'=8,'ctx'=4] {'dp'}, dimensions={0}, use_global_device_ids=true | all-gather | bytes 6912 | tf_op jit(solution)/shard_map/all_gather | solution.py:149
  185.3 20.6 %conditional.2 = (f32[1,12,256]{2,1,0:T(8,128)}, f32[1,12,256]{2,1,0:T(8,128)}, f32[1,256,12,64]{1,3,2,0:T(8,128)S(1)}, f32[1,12,256]{2,1,0:T(8,128)}) conditional(s32[]{:T(128)} %convert_element_type.249, () %tuple.48, (s32[256]{0:T(256)S(1)}, s32[1]{0:T(128)}, bf16[1,256,12,64]{1,3,2,0:T(8,128)(2,1)}, bf16[1,1024,768]{2,1,0:T(8,128)(2,1)}, ...), branch_computations={%region_2.0_spmd, %region_3.6_spmd} | conditional | flops 840431616 | bytes 106151000 | solution.py:188
  188.0 3.3 fusion.2
  191.9 4.1 fusion.4
  197.7 6.8 fusion.8
  210.5 36.0 %all-gather.21.cloned.1.call-done = bf16[768,3072]{1,0:T(8,128)(2,1)} async-done(((bf16[96,3072]{1,0:T(8,128)(2,1)}), bf16[768,3072]{1,0:T(8,128)(2,1)}) %all-gather.21.cloned.1.call-update) | async-done | bytes 4718608 | tf_op jit(solution)/shard_map/all_gather | solution.py:144
  246.5 12.3 %fusion.85 = (f32[256]{0:T(256)S(1)}, f32[256,3072]{1,0:T(8,128)S(1)}, f32[256,3072]{1,0:T(8,128)}, f32[256,3072]{1,0:T(8,128)}) fusion(f32[3072]{0:T(1024)S(1)} %bitcast.186, bf16[768,3072]{1,0:T(8,128)(2,1)} %all-gather.21.cloned.1.call-done, f32[256,768]{1,0:T(8,128)} %copy-done.6, f32[768]{0:T(1024)S(1)} %get-tuple-element.521, ...), kind=kOutput, calls=%fused_computation.178 | convolution fusion | flops 1260846848 | bytes 14963712 | tf_op jit(solution)/shard_map/dot_general | solution.py:205
  259.3 67.3 %all-gather.23.cloned.1.call-done = bf16[3072,768]{1,0:T(8,128)(2,1)} async-done(((bf16[384,768]{1,0:T(8,128)(2,1)}), bf16[3072,768]{1,0:T(8,128)(2,1)}) %all-gather.23.cloned.1.call-update) | async-done | bytes 4718608 | tf_op jit(solution)/shard_map/all_gather | solution.py:145
  326.6 5.8 convert_reduce_fusion.2
  337.5 3.2 fusion.78
  351.8 144.2 %while.24 = (s32[]{:T(128)}, bf16[1,256,768]{1,2,0:T(8,128)(2,1)}, bf16[1,256,768]{1,2,0:T(8,128)(2,1)}, f32[1,256,768]{1,2,0:T(8,128)}, f32[1,256,768]{1,2,0:T(...) while((s32[]{:T(128)}, bf16[1,256,768]{1,2,0:T(8,128)(2,1)}, ...), condition=%wide.region_25.26_spmd.clone, body=%wide.region_22.25_spmd.clone.sunk | while | flops 513672192 | bytes 48655496 | solution.py:269
  355.3 14.6 %conditional.5 = (f32[1,256,12,64]{1,3,2,0:T(8,128)}, f32[1,256,768]{1,2,0:T(8,128)}, f32[1,256,768]{1,2,0:T(8,128)}) conditional(s32[]{:T(128)} %convert_element_type.409, () %tuple.115, (s32[]{:T(128)}, s32[]{:T(128)}, s32[1]{0:T(128)}, bf16[1,256,12,64]{1,3,2,0:T(8,128)(2,1)}, bf16[1,256,768]{1,2,0:T(8,128)(2,1)S(1)}, ...), branch_computations={%region_23.23_spmd, %region_24.24_spmd} | conditional | flops 511706112 | bytes 32138860 | solution.py:257
  355.3 3.3 fusion.28
  360.0 3.5 multiply_convert_fusion
  367.3 2.7 fusion.18
  375.5 2.7 collective-permute-start
  390.1 2.8 conditional.5
  395.1 16.3 %collective-permute-start.2 = (bf16[1,256,768]{1,2,0:T(8,128)(2,1)}, bf16[1,256,768]{1,2,0:T(8,128)(2,1)}, u32[]{:S(2)}, u32[]{:S(2)}) collective-permute-start(bf16[1,256,768]{1,2,0:T(8,128)(2,1)} %fusion.110), channel_id=1, source_target_pairs={{0,1},{1,2},{2,3},{3,0},{4,5},{5,6},{6,7},{7,4},{8,9},{9,10},{10,1... | collective-permute-start | bytes 1179656 | tf_op jit(solution)/shard_map/while/body/eval_jaxpr/ppermute | solution.py:22
  416.1 2.7 collective-permute-start
  430.4 2.8 conditional.5
  435.4 4.5 collective-permute-start.2
  442.2 14.3 %collective-permute-start.3 = (bf16[1,256,768]{1,2,0:T(8,128)(2,1)}, bf16[1,256,768]{1,2,0:T(8,128)(2,1)}, u32[]{:S(2)}, u32[]{:S(2)}) collective-permute-start(bf16[1,256,768]{1,2,0:T(8,128)(2,1)} %fusion.111), channel_id=1, source_target_pairs={{0,1},{1,2},{2,3},{3,0},{4,5},{5,6},{6,7},{7,4},{8,9},{9,10},{10,1... | collective-permute-start | bytes 1179656 | tf_op jit(solution)/shard_map/while/body/eval_jaxpr/ppermute | solution.py:22
  456.5 2.7 collective-permute-start
  470.8 2.8 conditional.5
  475.8 4.5 collective-permute-start.2
  501.4 3.1 convolution_convert_fusion.2
  504.6 2.9 convolution_convert_fusion.3
  507.6 5.4 convolution_convert_fusion.1
  513.7 5.1 convolution_convert_fusion
  520.0 3.9 fusion.77
  541.7 45.7 %reduce-scatter.14.cloned.1.call-done = bf16[96,2304]{1,0:T(8,128)(2,1)} async-done(((bf16[768,2304]{1,0:T(8,128)(2,1)}), bf16[96,2304]{1,0:T(8,128)(2,1)}) %reduce-scatter.14.cloned.1.call-update) | async-done | bytes 442384 | tf_op jit(solution)/shard_map/reduce_scatter | solution.py:286
  589.3 65.6 %reduce-scatter.16.cloned.1.call-done = bf16[96,768]{1,0:T(8,128)(2,1)} async-done(((bf16[768,768]{1,0:T(8,128)(2,1)}), bf16[96,768]{1,0:T(8,128)(2,1)}) %reduce-scatter.16.cloned.1.call-update) | async-done | bytes 147472 | tf_op jit(solution)/shard_map/reduce_scatter | solution.py:289
  654.9 98.5 %reduce-scatter.18.cloned.1.call-done = bf16[96,3072]{1,0:T(8,128)(2,1)} async-done(((bf16[768,3072]{1,0:T(8,128)(2,1)}), bf16[96,3072]{1,0:T(8,128)(2,1)}) %reduce-scatter.18.cloned.1.call-update) | async-done | bytes 589840 | tf_op jit(solution)/shard_map/reduce_scatter | solution.py:292
  753.4 98.5 %reduce-scatter.20.cloned.1.call-done = bf16[384,768]{1,0:T(8,128)(2,1)} async-done(((bf16[3072,768]{1,0:T(8,128)(2,1)}), bf16[384,768]{1,0:T(8,128)(2,1)}) %reduce-scatter.20.cloned.1.call-update) | async-done | bytes 589840 | tf_op jit(solution)/shard_map/reduce_scatter | solution.py:295
  856.5 40.6 %all-reduce.3 = (f32[]{:T(128)}, f32[]{:T(128)}) all-reduce(f32[]{:T(128)S(6)} %mul.346, f32[]{:T(128)} %fusion.71), channel_id=1, replica_groups=mesh['dp'=8,'ctx'=4] {'dp','ctx'}, use_global_device_ids=true, to_apply=%region_13.14 | all-reduce | flops 2 | bytes 16 | tf_op jit(solution)/shard_map/psum | solution.py:215
  897.0 36.7 %all-reduce.4 = (bf16[3072]{0:T(1024)(128)(2,1)S(1)}, bf16[3072]{0:T(1024)(128)(2,1)S(1)}, bf16[3072]{0:T(1024)(128)(2,1)S(1)}) all-reduce(bf16[3072]{0:T(1024)(128)(2,1)} %get-tuple-element.504, bf16[3072]{0:T(1024)(128)(2,1)} %get-tuple-element.506, bf16[3072]{0:T(1024)(128)(2,1)S(1)} %copy-done.38), channel_id=12, replica_groups=mesh['dp'=8,'ctx'=4] {'dp'}, use_global_device_ids=true, to_apply=%region_53.54.clone | all-reduce | flops 9216 | bytes 36864
  937.6 43.0 %reduce-scatter.24.cloned.1.call-done = bf16[96,3]{1,0:T(8,128)(2,1)} async-done(((bf16[768,3]{1,0:T(8,128)(2,1)}), bf16[96,3]{1,0:T(8,128)(2,1)}) %reduce-scatter.24.cloned.1.call-update) | async-done | bytes 592
  981.4 62.6 %reduce-scatter.26.cloned.1.call-done = bf16[96,4]{1,0:T(8,128)(2,1)} async-done(((bf16[768,4]{1,0:T(8,128)(2,1)}), bf16[96,4]{1,0:T(8,128)(2,1)}) %reduce-scatter.26.cloned.1.call-update) | async-done | bytes 784
  1044.8 5.7 all-reduce.5
  1054.0 11.2 all-gather.29.cloned.1.call-done
  1067.9 39.4 %all-reduce.9.cloned.1.call-done = (bf16[96,768]{1,0:T(8,128)(2,1)}, bf16[96,3072]{1,0:T(8,128)(2,1)}, bf16[384,768]{1,0:T(8,128)(2,1)}) async-done(((bf16[96,768]{1,0:T(8,128)(2,1)}, bf16[96,3072]{1,0:T(8,128)(2,1)}, bf16[384,768]{1,0:T(8,128)(2,1)}), (bf16[96,768]{1,0:T(8,128)(2,1)}, bf16[96,3072]{1,0:T(8,128)(2,1)}, bf16[384,768]{1,0:T(8,128)(2,1)})) %all-reduce.9.cloned.1.call-update) | async-done | bytes 1327120 | tf_op jit(solution)/shard_map/psum | solution.py:319
  (346 shorter events, 170.6 us)
Async XLA Ops:
  7.2 71.0 %all-gather.17.cloned.1.call-start = ((), (), s32[]{:S(2)}) async-start(), calls=%async_computation.7 | async-start | bytes 3981312 | tf_op jit(solution)/shard_map/all_gather | solution.py:142
  7.9 177.4 %all-gather.25.cloned.1.call-start = ((), (), s32[]{:S(2)}) async-start(), calls=%async_computation.15 | async-start | bytes 1966080 | tf_op jit(solution)/shard_map/all_gather | solution.py:184
  47.4 159.9 %copy-start.43 = (f32[768]{0:T(1024)}, f32[768]{0:T(1024)S(1)}, u32[]{:S(2)}) copy-start(f32[768]{0:T(1024)S(1)} %get-tuple-element.522) | copy-start | bytes 9220
  47.4 199.0 %copy-start.31 = (f32[768]{0:T(1024)}, f32[768]{0:T(1024)S(1)}, u32[]{:S(2)}) copy-start(f32[768]{0:T(1024)S(1)} %get-tuple-element.521) | copy-start | bytes 9220
  47.4 299.6 %copy-start.32 = (f32[768]{0:T(1024)}, f32[768]{0:T(1024)S(1)}, u32[]{:S(2)}) copy-start(f32[768]{0:T(1024)S(1)} %get-tuple-element.604) | copy-start | bytes 9220
  81.6 74.5 %copy-start.62 = (bf16[384]{0:T(512)(128)(2,1)S(1)}, bf16[384]{0:T(512)(128)(2,1)}, u32[]{:S(2)}) copy-start(bf16[384]{0:T(512)(128)(2,1)} %param.29) | copy-start | bytes 2308
  82.4 102.9 %all-gather.27.cloned.1.call-start = ((), (), s32[]{:S(2)}) async-start(), calls=%async_computation.16 | async-start | bytes 1966080 | tf_op jit(solution)/shard_map/all_gather | solution.py:185
  101.6 82.9 %copy-start.16 = (bf16[256,768]{1,0:T(8,128)(2,1)S(1)}, bf16[256,768]{1,0:T(8,128)(2,1)}, u32[]{:S(2)}) copy-start(bf16[256,768]{1,0:T(8,128)(2,1)} %get-tuple-element.591) | copy-start | bytes 1179652
  101.6 105.8 %all-gather.19.cloned.1.call-start = ((), (), s32[]{:S(2)}) async-start(), calls=%async_computation.8 | async-start | bytes 1327104 | tf_op jit(solution)/shard_map/all_gather | solution.py:143
  102.2 144.3 %all-gather.21.cloned.1.call-start = ((), (), s32[]{:S(2)}) async-start(), calls=%async_computation.9 | async-start | bytes 5308416 | tf_op jit(solution)/shard_map/all_gather | solution.py:144
  102.7 223.8 %all-gather.23.cloned.1.call-start = ((), (), s32[]{:S(2)}) async-start(), calls=%async_computation.10 | async-start | bytes 5308416 | tf_op jit(solution)/shard_map/all_gather | solution.py:145
  103.3 484.1 %reduce-scatter.14.cloned.1.call-start = ((), (), s32[]{:S(2)}) async-start(), calls=%async_computation.11 | async-start | bytes 3981312 | tf_op jit(solution)/shard_map/reduce_scatter | solution.py:286
  156.1 170.4 %copy-start.28 = (f32[8,1,384]{2,1,0:T(1,128)}, f32[8,1,384]{2,1,0:T(1,128)S(1)}, u32[]{:S(2)}) copy-start(f32[8,1,384]{2,1,0:T(1,128)S(1)} %convert_element_type.302) | copy-start | bytes 36868
  182.5 144.0 %copy-start.56 = (f32[256]{0:T(256)}, f32[256]{0:T(256)S(1)}, u32[]{:S(2)}) copy-start(f32[256]{0:T(256)S(1)} %compare_convert_fusion) | copy-start | bytes 3076
  207.1 139.9 %copy-start.42 = (f32[256]{0:T(256)}, f32[256]{0:T(256)S(1)}, u32[]{:S(2)}) copy-start(f32[256]{0:T(256)S(1)} %broadcast_multiply_fusion.2) | copy-start | bytes 3076
  207.3 139.7 %copy-start.51 = (f32[256]{0:T(256)}, f32[256]{0:T(256)S(1)}, u32[]{:S(2)}) copy-start(f32[256]{0:T(256)S(1)} %fusion.63) | copy-start | bytes 3076
  209.3 134.8 %copy-start.37 = (f32[256]{0:T(256)}, f32[256]{0:T(256)S(1)}, u32[]{:S(2)}) copy-start(f32[256]{0:T(256)S(1)} %broadcast_multiply_fusion.1) | copy-start | bytes 3076
  210.4 133.7 %copy-start.45 = (f32[256]{0:T(256)}, f32[256]{0:T(256)S(1)}, u32[]{:S(2)}) copy-start(f32[256]{0:T(256)S(1)} %fusion.64) | copy-start | bytes 3076
  258.8 77.7 %copy-start.29 = (f32[256]{0:T(256)}, f32[256]{0:T(256)S(1)}, u32[]{:S(2)}) copy-start(f32[256]{0:T(256)S(1)} %broadcast_multiply_fusion) | copy-start | bytes 3076
  259.3 77.2 %copy-start.36 = (f32[256]{0:T(256)}, f32[256]{0:T(256)S(1)}, u32[]{:S(2)}) copy-start(f32[256]{0:T(256)S(1)} %fusion.65) | copy-start | bytes 3076
  371.9 10.9 collective-permute-start.2
  373.9 10.9 collective-permute-start.3
  375.5 11.2 %collective-permute-start = (bf16[1,256,768]{1,2,0:T(8,128)(2,1)S(1)}, bf16[1,256,768]{1,2,0:T(8,128)(2,1)}, u32[]{:S(2)}, u32[]{:S(2)}) collective-permute-start(bf16[1,256,768]{1,2,0:T(8,128)(2,1)S(1)} %copy.106), channel_id=1, source_target_pairs={{0,1},{1,2},{2,3},{4,5},{5,6},{6,7},{8,9},{9,10},{10,11},{12,13},{... | collective-permute-start | bytes 1179656 | tf_op jit(solution)/shard_map/while/body/eval_jaxpr/ppermute | solution.py:28
  378.2 8.6 collective-permute-start.1
  395.1 28.0 %collective-permute-start.2 = (bf16[1,256,768]{1,2,0:T(8,128)(2,1)}, bf16[1,256,768]{1,2,0:T(8,128)(2,1)}, u32[]{:S(2)}, u32[]{:S(2)}) collective-permute-start(bf16[1,256,768]{1,2,0:T(8,128)(2,1)} %fusion.110), channel_id=1, source_target_pairs={{0,1},{1,2},{2,3},{3,0},{4,5},{5,6},{6,7},{7,4},{8,9},{9,10},{10,1... | collective-permute-start | bytes 1179656 | tf_op jit(solution)/shard_map/while/body/eval_jaxpr/ppermute | solution.py:22
  413.6 11.5 %collective-permute-start.3 = (bf16[1,256,768]{1,2,0:T(8,128)(2,1)}, bf16[1,256,768]{1,2,0:T(8,128)(2,1)}, u32[]{:S(2)}, u32[]{:S(2)}) collective-permute-start(bf16[1,256,768]{1,2,0:T(8,128)(2,1)} %fusion.111), channel_id=1, source_target_pairs={{0,1},{1,2},{2,3},{3,0},{4,5},{5,6},{6,7},{7,4},{8,9},{9,10},{10,1... | collective-permute-start | bytes 1179656 | tf_op jit(solution)/shard_map/while/body/eval_jaxpr/ppermute | solution.py:22
  416.1 10.9 collective-permute-start
  418.8 8.3 collective-permute-start.1
  435.4 28.1 %collective-permute-start.2 = (bf16[1,256,768]{1,2,0:T(8,128)(2,1)}, bf16[1,256,768]{1,2,0:T(8,128)(2,1)}, u32[]{:S(2)}, u32[]{:S(2)}) collective-permute-start(bf16[1,256,768]{1,2,0:T(8,128)(2,1)} %fusion.110), channel_id=1, source_target_pairs={{0,1},{1,2},{2,3},{3,0},{4,5},{5,6},{6,7},{7,4},{8,9},{9,10},{10,1... | collective-permute-start | bytes 1179656 | tf_op jit(solution)/shard_map/while/body/eval_jaxpr/ppermute | solution.py:22
  442.2 23.3 %collective-permute-start.3 = (bf16[1,256,768]{1,2,0:T(8,128)(2,1)}, bf16[1,256,768]{1,2,0:T(8,128)(2,1)}, u32[]{:S(2)}, u32[]{:S(2)}) collective-permute-start(bf16[1,256,768]{1,2,0:T(8,128)(2,1)} %fusion.111), channel_id=1, source_target_pairs={{0,1},{1,2},{2,3},{3,0},{4,5},{5,6},{6,7},{7,4},{8,9},{9,10},{10,1... | collective-permute-start | bytes 1179656 | tf_op jit(solution)/shard_map/while/body/eval_jaxpr/ppermute | solution.py:22
  456.5 10.9 collective-permute-start
  459.2 8.3 collective-permute-start.1
  475.8 16.3 %collective-permute-start.2 = (bf16[1,256,768]{1,2,0:T(8,128)(2,1)}, bf16[1,256,768]{1,2,0:T(8,128)(2,1)}, u32[]{:S(2)}, u32[]{:S(2)}) collective-permute-start(bf16[1,256,768]{1,2,0:T(8,128)(2,1)} %fusion.110), channel_id=1, source_target_pairs={{0,1},{1,2},{2,3},{3,0},{4,5},{5,6},{6,7},{7,4},{8,9},{9,10},{10,1... | collective-permute-start | bytes 1179656 | tf_op jit(solution)/shard_map/while/body/eval_jaxpr/ppermute | solution.py:22
  482.6 11.5 %collective-permute-start.3 = (bf16[1,256,768]{1,2,0:T(8,128)(2,1)}, bf16[1,256,768]{1,2,0:T(8,128)(2,1)}, u32[]{:S(2)}, u32[]{:S(2)}) collective-permute-start(bf16[1,256,768]{1,2,0:T(8,128)(2,1)} %fusion.111), channel_id=1, source_target_pairs={{0,1},{1,2},{2,3},{3,0},{4,5},{5,6},{6,7},{7,4},{8,9},{9,10},{10,1... | collective-permute-start | bytes 1179656 | tf_op jit(solution)/shard_map/while/body/eval_jaxpr/ppermute | solution.py:22
  485.1 10.9 collective-permute-start
  487.7 8.3 collective-permute-start.1
  504.6 150.3 %reduce-scatter.16.cloned.1.call-start = ((), (), s32[]{:S(2)}) async-start(), calls=%async_computation.12 | async-start | bytes 1327104 | tf_op jit(solution)/shard_map/reduce_scatter | solution.py:289
  507.6 245.8 %reduce-scatter.18.cloned.1.call-start = ((), (), s32[]{:S(2)}) async-start(), calls=%async_computation.13 | async-start | bytes 5308416 | tf_op jit(solution)/shard_map/reduce_scatter | solution.py:292
  513.0 338.9 %reduce-scatter.20.cloned.1.call-start = ((), (), s32[]{:S(2)}) async-start(), calls=%async_computation.14 | async-start | bytes 5308416 | tf_op jit(solution)/shard_map/reduce_scatter | solution.py:295
  518.8 418.0 %reduce-scatter.22.cloned.1.call-start = ((), (), s32[]{:S(2)}) async-start(), calls=%async_computation.18 | async-start | bytes 221184
  523.9 328.7 %copy-start.5 = (f32[256,768]{1,0:T(8,128)S(1)}, f32[256,768]{1,0:T(8,128)}, u32[]{:S(2)}) copy-start(f32[256,768]{1,0:T(8,128)} %copy-done.4) | copy-start | bytes 2359300
  523.9 328.7 %copy-start.9 = (f32[256,768]{1,0:T(8,128)S(1)}, f32[256,768]{1,0:T(8,128)}, u32[]{:S(2)}) copy-start(f32[256,768]{1,0:T(8,128)} %copy-done.8) | copy-start | bytes 2359300
  530.5 366.6 %copy-start.38 = (bf16[3072]{0:T(1024)(128)(2,1)S(1)}, bf16[3072]{0:T(1024)(128)(2,1)}, u32[]{:S(2)}) copy-start(bf16[3072]{0:T(1024)(128)(2,1)} %get-tuple-element.568) | copy-start | bytes 18436
  530.5 404.8 %copy-start.21 = (f32[256,768]{1,0:T(8,128)S(1)}, f32[256,768]{1,0:T(8,128)}, u32[]{:S(2)}) copy-start(f32[256,768]{1,0:T(8,128)} %get-tuple-element.598) | copy-start | bytes 2359300
  530.5 450.1 %reduce-scatter.24.cloned.1.call-start = ((), (), s32[]{:S(2)}) async-start(), calls=%async_computation.19 | async-start | bytes 221184
  538.8 505.2 %reduce-scatter.26.cloned.1.call-start = ((), (), s32[]{:S(2)}) async-start(), calls=%async_computation.20 | async-start | bytes 221184
  541.7 523.5 %all-gather.29.cloned.1.call-start = ((), (), s32[]{:S(2)}) async-start(), calls=%async_computation.17 | async-start | bytes 2211840 | tf_op jit(solution)/shard_map/all_gather | solution.py:14
  587.4 520.0 %all-reduce.9.cloned.1.call-start = ((), (), s32[]{:S(2)}) async-start(), calls=%async_computation.21 | async-start | bytes 2654208 | tf_op jit(solution)/shard_map/psum | solution.py:319
  (49 other events, 412.1 us)
Sparse Core Ops, SparseCore 0:
  10.2 67.9 all-gather.16
  82.5 18.1 all-gather.24
  102.9 19.6 all-gather.26
  124.6 41.1 all-gather.18
  167.8 78.6 all-gather.20
  248.5 78.0 all-gather.22
  504.7 82.6 reduce-scatter.13
  591.3 63.5 reduce-scatter.15
  658.6 94.7 reduce-scatter.17
  756.9 94.9 reduce-scatter.19
  855.7 60.8 reduce-scatter.21
  920.3 60.1 reduce-scatter.23
  983.8 60.1 reduce-scatter.25
  1045.4 19.7 all-gather.28
  1067.6 39.7 all-reduce.8
